TPU v7x, 256 devices: a whole 4x4x8 slice. The times are simulated.
256 devices in a mesh: pb: 64 (over x, z, core), ka: 4 (over y).
Axes of the slice: x: 4, y: 4, z: 8, core: 2. Of those that a mesh axis runs over, the one named last changes fastest.
Arguments:
- valence: float32 [1664, 64, 1024], P('pb', 'ka'), may hold values from -6 to 6
- conduction: bfloat16 [1664, 196, 1024], P('pb', None, 'ka'), may hold values from -0.0024414062 to 0.0024414062
- screened: float32 [64, 1024, 1024], P('pb'), may hold values from -1 to 3, as said below
- momentum: int32 [1664, 1], P('pb'), may hold values from 0 to 63; in each aligned block of 26 rows (0 to 25, 26 to 51, ...) at most 2 rows name the same one
- kpairs: int32 [1664, 2], P('pb'), may hold values from 0 to 63
- kpoint_slot: int32 [64], replicated, may hold values from 0 to 63, each once
- trial_blocks: float32 [64, 14336], P('pb', 'ka'), may hold values from -6 to 6
Outputs:
- response: float32 [64, 14336], P('pb', 'ka')
Inputs may be any that keep to these rules, and one draw needn't show every extreme that they name: Among the k-pairs of one index of pb (rows i * 26 to (i + 1) * 26 - 1), at most 2 share a momentum transfer. `kpoint_slot`: each row number appears once. `screened`: each matrix is symmetric.
All inputs are finite; a program needn't handle non-finite values.
Results may differ from a plain program's by a relative error of at most 0.0003.
Values sent between devices are 32-bit elements; how exact they have to be, the bound alone decides.
No kernel may reach another device: no remote copies, remote signals or barrier semaphores. Data moves between devices by JAX's collectives and lax.ppermute only.
A program may use at most 128 MiB of HBM per device.

v0:
```python
import jax
import jax.numpy as jnp
from jax import lax
from jax.sharding import PartitionSpec as P

VB = 8
CB = 14


def local(valence, conduction, screened, momentum, kpairs, kpoint_slot, trial_blocks):
    highest = lax.Precision.HIGHEST
    pair_dev = valence.shape[0]
    owners = lax.axis_size("pb")
    capacity = max(2, 2 * pair_dev // owners)
    slot_count = owners * capacity
    target = momentum[:, 0]
    indices = jnp.arange(pair_dev, dtype=jnp.int32)
    earlier = (target[:, None] == target[None, :]) & (indices[None, :] < indices[:, None])
    position = target * capacity + jnp.sum(earlier.astype(jnp.int32), axis=1)
    matches = position[None, :] == jnp.arange(slot_count, dtype=jnp.int32)[:, None]
    source = jnp.sum(jnp.where(matches, indices[None, :], 0), axis=1)
    filled = jnp.any(matches, axis=1)
    outgoing = jnp.where(filled[:, None, None], jnp.take(valence, source, axis=0), 0.0)
    outgoing = outgoing.reshape(owners, capacity, valence.shape[1], valence.shape[2])
    matrix = screened[0]
    product = jnp.einsum(
        "scrg,gh->scrh",
        lax.all_to_all(outgoing, "pb", split_axis=0, concat_axis=0, tiled=True),
        matrix,
        precision=highest,
        preferred_element_type=jnp.float32,
    )
    returned = lax.all_to_all(
        lax.all_to_all(product, "pb", split_axis=0, concat_axis=0, tiled=True),
        "ka",
        split_axis=3,
        concat_axis=2,
        tiled=True,
    )
    by_slot = returned.reshape(slot_count, returned.shape[2], returned.shape[3])
    columns = jnp.take(by_slot, position, axis=0)
    conduct_wide = conduction.astype(jnp.float32)
    partial_kernel = jnp.einsum(
        "prg,pbg->prb", columns, conduct_wide, precision=highest, preferred_element_type=jnp.float32
    )
    kernel = lax.psum(partial_kernel, "ka")
    gathered = lax.all_gather(trial_blocks, "pb", axis=0, tiled=True)
    kpoint_count = gathered.shape[0]
    local_trials = gathered.shape[1] // (VB * CB)
    blocks = gathered.reshape(kpoint_count, local_trials, VB, CB)
    slot_near = jnp.take(kpoint_slot, kpairs[:, 0])
    slot_far = jnp.take(kpoint_slot, kpairs[:, 1])
    near_trials = jnp.take(blocks, slot_near, axis=0)
    far_trials = jnp.take(blocks, slot_far, axis=0)
    kernel_blocks = kernel.reshape(pair_dev, VB, VB, CB, CB)
    direct = jnp.einsum("pvwcd,pnwd->pnvc", kernel_blocks, far_trials, precision=highest)
    mirror = jnp.einsum("pvwcd,pnvc->pnwd", kernel_blocks, near_trials, precision=highest)
    kpoint_rows = jnp.arange(kpoint_count, dtype=jnp.int32)[:, None]
    onehot_near = (slot_near[None, :] == kpoint_rows).astype(jnp.float32)
    onehot_far = (slot_far[None, :] == kpoint_rows).astype(jnp.float32)
    summed = jnp.dot(
        onehot_near,
        direct.reshape(pair_dev, -1),
        precision=highest,
        preferred_element_type=jnp.float32,
    )
    summed = summed + jnp.dot(
        onehot_far,
        mirror.reshape(pair_dev, -1),
        precision=highest,
        preferred_element_type=jnp.float32,
    )
    return lax.psum_scatter(summed, "pb", scatter_dimension=0, tiled=True)


def solution(mesh):
    return jax.shard_map(
        local,
        mesh=mesh,
        in_specs=(
            P("pb", "ka", None),
            P("pb", None, "ka"),
            P("pb", None, None),
            P("pb", None),
            P("pb", None),
            P(),
            P("pb", "ka"),
        ),
        out_specs=P("pb", "ka"),
        check_vma=False,
    )
```

profile of v0, /device:TPU:8, one launch (start us, length us, event | category | flops | bytes accessed | tf_op | source)
XLA Modules:
  0.0 1163.5 jit_solution(17893508544063465319)
XLA Ops:
  6.5 0.0 copy-start
  6.5 1.0 convert_reduce_fusion
  7.5 0.7 multiply_add_fusion
  8.2 0.1 select_reduce_fusion
  8.3 0.1 fusion.16
  8.4 0.1 reduce_sum.27
  8.5 0.1 broadcast_in_dim.68
  8.7 5.8 gather_fusion
  14.5 4.0 select_select_fusion
  18.4 0.0 copy-start.5
  18.5 198.0 %all_to_all.25 = f32[64,2,16,1024]{3,2,1,0:T(8,128)S(1)} all-to-all(f32[64,2,16,1024]{3,2,1,0:T(8,128)S(1)} %select_select_fusion), channel_id=1, replica_groups=mesh['pb'=64,'ka'=4] {'pb'}, dimensions={0} | all-to-all | bytes 16777216 | tf_op jit(solution)/shard_map/all_to_all | solution.py:28
  216.4 0.0 copy-done.5
  216.4 27.7 %fusion = f32[64,2,16,1024]{3,2,1,0:T(8,128)S(1)} fusion(f32[64,2,16,1024]{3,2,1,0:T(8,128)S(1)} %all_to_all.25, f32[1,1024,1024]{2,1,0:T(8,128)S(1)} %copy-done.5), kind=kOutput, calls=%fused_computation.8 | convolution fusion | flops 25769803776 | bytes 20971520 | tf_op jit(solution)/shard_map/scrg,gh->scrh/dot_general | solution.py:26
  244.1 192.1 %all_to_all.26 = f32[64,2,16,1024]{3,2,1,0:T(8,128)} all-to-all(f32[64,2,16,1024]{3,2,1,0:T(8,128)S(1)} %fusion), channel_id=1, replica_groups=mesh['pb'=64,'ka'=4] {'pb'}, dimensions={0} | all-to-all | bytes 16777216 | tf_op jit(solution)/shard_map/all_to_all | solution.py:34
  436.2 16.3 %copy.61 = f32[64,2,16,1024]{0,2,1,3:T(8,128)} copy(f32[64,2,16,1024]{3,2,1,0:T(8,128)} %all_to_all.26) | data formatting | bytes 16777216 | tf_op jit(solution)/shard_map/all_to_all | solution.py:34
  452.5 14.3 %reshape.142 = f32[4,1,524288]{2,1,0:T(1,128)} reshape(f32[1024,2,16,64]{3,2,1,0:T(8,128)} %bitcast.68) | data formatting | bytes 16777216
  466.8 0.0 copy-start.4
  466.8 6.2 all-to-all-start.2
  473.0 0.0 all-reduce.4.cloned.1.call-start
  473.0 0.0 copy-done.4
  473.0 92.9 %all-to-all-done.2 = f32[4,1,524288]{2,1,0:T(1,128)} async-done(((f32[4,1,524288]{2,1,0:T(1,128)}), f32[4,1,524288]{2,1,0:T(1,128)}, u32[]{:S(2)}, u32[]{:S(2)}) %all-to-all-start.2) | async-done | bytes 8388640 | tf_op jit(solution)/shard_map/all_to_all | solution.py:33
  566.0 0.5 broadcast.181
  566.5 30.1 %reduce = f32[4,524288]{1,0:T(4,128)} reduce(f32[4,1,524288]{2,1,0:T(1,128)} %all-to-all-done.2, f32[]{:T(128)} %broadcast.181), dimensions={1}, to_apply=%all_to_all.19.reduce_sub_computation | reduce | bytes 16777220 | tf_op jit(solution)/shard_map/all_to_all | solution.py:33
  596.6 16.8 %reshape.143 = f32[1024,2,16,64]{3,2,1,0:T(8,128)} reshape(f32[4,524288]{1,0:T(4,128)} %reduce) | data formatting | bytes 16777216
  613.4 14.4 %copy.75 = f32[64,2,16,4,256]{4,3,2,1,0:T(4,128)} copy(f32[64,2,16,4,256]{0,2,1,4,3:T(8,128)} %bitcast.69) | data formatting | bytes 16777216 | tf_op jit(solution)/shard_map/all_to_all | solution.py:33
  627.8 8.6 copy.63
  636.4 5.3 gather_fusion.1
  641.7 0.0 copy-done
  641.7 5.3 fusion.2
  647.0 5.8 copy.64
  652.8 14.5 %copy.65 = f32[26,8,8,14,14]{3,2,4,1,0:T(8,128)} copy(f32[26,8,8,14,14]{0,2,1,4,3:T(8,128)} %bitcast.72) | data formatting | bytes 2609152 | tf_op jit(solution)/shard_map/reshape | solution.py:55
  667.3 0.0 copy-start.3
  667.3 0.0 copy-start.1
  667.3 0.0 copy-start.2
  667.3 0.0 all-reduce.4.cloned.1.call-update
  667.3 0.0 all-reduce.6.cloned.1.call-start
  667.4 0.6 copy-done.3
  668.0 0.0 copy-done.1
  668.0 0.7 gather_fusion.3
  668.7 0.7 gather_fusion.2
  669.4 0.0 copy-done.2
  669.4 52.6 %all-gather = f32[64,1,3584]{2,1,0:T(1,128)} all-gather(f32[1,1,3584]{2,1,0:T(1,128)S(1)} %bitcast.74), channel_id=1, replica_groups=mesh['pb'=64,'ka'=4] {'pb'}, dimensions={0}, use_global_device_ids=true | all-gather | bytes 931840 | tf_op jit(solution)/shard_map/all_gather | solution.py:47
  722.0 4.1 copy.59
  726.1 2.7 reshape.68
  728.7 5.5 copy.60
  734.2 3.9 gather_fusion.5
  738.1 3.8 gather_fusion.4
  741.9 142.4 %all-reduce.4.cloned.1.call-done = f32[26,8,8,14,14]{3,2,4,1,0:T(8,128)} async-done(((f32[26,8,8,14,14]{3,2,4,1,0:T(8,128)}), f32[26,8,8,14,14]{3,2,4,1,0:T(8,128)}) %all-reduce.4.cloned.1.call-update) | async-done | bytes 1304592 | tf_op jit(solution)/shard_map/psum | solution.py:46
  884.3 16.3 %copy.68 = f32[26,8,8,14,14]{4,1,3,2,0:T(8,128)} copy(f32[26,8,8,14,14]{3,2,4,1,0:T(8,128)} %all-reduce.4.cloned.1.call-done) | data formatting | bytes 2609152 | tf_op jit(solution)/shard_map/psum | solution.py:46
  900.7 22.8 %convolution_bitcast_fusion = f32[26,32,8,14]{1,3,2,0:T(8,128)} fusion(f32[26,8,8,14,14]{4,1,3,2,0:T(8,128)} %copy.68, f32[26,32,8,14]{1,2,3,0:T(8,128)} %gather_fusion.5, pred[26]{0:T(512)(128)(4,1)S(1)} %get-tuple-element.6), kind=kOutput, calls=%fused_computation.12 | convolution fusion | flops 125332480 | bytes 2050074 | tf_op jit(solution)/shard_map/pvwcd,pnvc->pnwd/dot_general | solution.py:57
  923.5 3.7 copy.69
  927.2 4.0 reshape.72
  931.2 23.0 %convolution_bitcast_fusion.1 = f32[26,32,8,14]{1,3,2,0:T(8,128)} fusion(f32[26,8,8,14,14]{3,2,4,1,0:T(8,128)} %all-reduce.4.cloned.1.call-done, f32[26,32,8,14]{1,2,3,0:T(8,128)} %gather_fusion.4, pred[26]{0:T(512)(128)(4,1)S(1)} %get-tuple-element.13), kind=kOutput, calls=%fused_computation.13 | convolution fusion | flops 125332480 | bytes 2050074 | tf_op jit(solution)/shard_map/pvwcd,pnwd->pnvc/dot_general | solution.py:56
  954.2 3.7 copy.66
  957.9 0.0 copy-start.6
  957.9 4.6 reshape.71
  962.5 1.5 fusion.14
  964.0 1.5 convolution_add_fusion
  965.5 0.0 all-reduce.6.cloned.1.call-update
  965.5 0.0 copy-done.6
  965.5 0.7 dynamic-slice
  966.2 188.0 %all-reduce.6.cloned.1.call-done = f32[64,3584]{1,0:T(8,128)} async-done(((f32[64,3584]{1,0:T(8,128)}), f32[64,3584]{1,0:T(8,128)}) %all-reduce.6.cloned.1.call-update) | async-done | bytes 917520
  1154.2 2.2 constant_dynamic-slice_fusion
  (12 shorter events, 0.1 us)
Async XLA Ops:
  6.5 635.1 %copy-start = (bf16[26,196,256]{2,1,0:T(8,128)(2,1)S(1)}, bf16[26,196,256]{2,1,0:T(8,128)(2,1)}, u32[]{:S(2)}) copy-start(bf16[26,196,256]{2,1,0:T(8,128)(2,1)} %param.12) | copy-start | bytes 7827460
  18.4 198.0 %copy-start.5 = (f32[1,1024,1024]{2,1,0:T(8,128)S(1)}, f32[1,1024,1024]{2,1,0:T(8,128)}, u32[]{:S(2)}) copy-start(f32[1,1024,1024]{2,1,0:T(8,128)} %param.13) | copy-start | bytes 12582916
  466.8 6.2 copy-start.4
  466.8 99.1 %all-to-all-start.2 = ((f32[4,1,524288]{2,1,0:T(1,128)}), f32[4,1,524288]{2,1,0:T(1,128)}, u32[]{:S(2)}, u32[]{:S(2)}) async-start(f32[4,1,524288]{2,1,0:T(1,128)} %reshape.142), calls=%async_computation.2 | async-start | bytes 16777216 | tf_op jit(solution)/shard_map/all_to_all | solution.py:33
  473.0 411.3 %all-reduce.4.cloned.1.call-start = ((), (), s32[]{:S(2)}) async-start(), calls=%async_computation.3 | async-start | bytes 23855104 | tf_op jit(solution)/shard_map/psum | solution.py:46
  667.3 0.7 copy-start.3
  667.3 0.7 copy-start.1
  667.3 2.1 copy-start.2
  667.3 486.9 %all-reduce.6.cloned.1.call-start = ((), (), s32[]{:S(2)}) async-start(), calls=%async_computation.4 | async-start | bytes 1835008
  957.9 7.6 copy-start.6
Sparse Core Ops, SparseCore 0:
  667.4 216.8 all-reduce.3
  965.7 188.5 all-reduce.5
where the time goes:
time: 1170 us; the launch traced here: 1160 us
  blocking collectives  443 us (38%)
  waiting for transfers between devices  423 us (36%)
  local copies, waits for them, and re-layouts  160 us (14%)
  matrix products  81.8 us (7%)
  other arithmetic  36 us (3%)
  between operations  13.8 us (1%)
    all_to_all x1, blocking collectives, local(): lax.all_to_all(outgoing, 'pb', split_axis=0, concat_axis=0, tiled=True)  198 us
    all_to_all x1, blocking collectives, local(): lax.all_to_all(product, 'pb', split_axis=0, concat_axis=0, tiled=True)  192 us
    unnamed x3, waiting for transfers between devices  188 us
    psum x1, waiting for transfers between devices, local(): kernel = lax.psum(partial_kernel, 'ka')  142 us
    all_to_all x1, waiting for transfers between devices, local(): lax.all_to_all(lax.all_to_all(product, 'pb', split_axis=0, concat_axis=0,...  92.9 us
    all_gather x1, blocking collectives, local(): gathered = lax.all_gather(trial_blocks, 'pb', axis=0, tiled=True)  52.6 us
    unnamed x18, local copies, waits for them, and re-layouts  34.6 us
    all_to_all x1, other arithmetic, local(): lax.all_to_all(lax.all_to_all(product, 'pb', split_axis=0, concat_axis=0,...  30.1 us
  transfers between devices with their start and end apart: 3, of which 3 were waited for; matrix products, arithmetic and copies ran while one was open for 2% of the time, Pallas kernels for 0%

commit v1 on v0

--- a/solution.py
+++ b/solution.py
@@ -43,7 +43,8 @@
     partial_kernel = jnp.einsum(
         "prg,pbg->prb", columns, conduct_wide, precision=highest, preferred_element_type=jnp.float32
     )
-    kernel = lax.psum(partial_kernel, "ka")
+    pieces = lax.all_gather(partial_kernel, "ka", axis=0, tiled=False)
+    kernel = pieces.sum(axis=0)
     gathered = lax.all_gather(trial_blocks, "pb", axis=0, tiled=True)
     kpoint_count = gathered.shape[0]
     local_trials = gathered.shape[1] // (VB * CB)

time: 1170 us -> 1040 us (0.89)
  waiting for transfers between devices: 423 us -> 277 us
    psum x1 -> x0, waiting for transfers between devices: 142 us -> none  [local(): kernel = lax.psum(partial_kernel, 'ka')]
    psum x1 -> x0, local copies, waits for them, and re-layouts: 16.3 us -> none  [local(): kernel = lax.psum(partial_kernel, 'ka')]
    reshape x1 -> x2, local copies, waits for them, and re-layouts: 14.5 us -> 29.1 us  [local(): kernel_blocks = kernel.reshape(pair_dev, VB, VB, CB, CB)]
  transfers between devices with their start and end apart: 3 -> 3, of which waited for: 3 -> 2; matrix products, arithmetic and copies ran while one was open for 2% -> 2% of each run, Pallas kernels for 0% -> 0%
where the time goes in v1:
time: 1040 us; the launch traced here: 1030 us
  blocking collectives  442 us (42%)
  waiting for transfers between devices  277 us (27%)
  local copies, waits for them, and re-layouts  165 us (16%)
  matrix products  83.2 us (8%)
  other arithmetic  41.1 us (4%)
  between operations  14 us (1%)
    all_to_all x1, blocking collectives, local(): lax.all_to_all(outgoing, 'pb', split_axis=0, concat_axis=0, tiled=True)  198 us
    all_to_all x1, blocking collectives, local(): lax.all_to_all(product, 'pb', split_axis=0, concat_axis=0, tiled=True)  192 us
    unnamed x3, waiting for transfers between devices  184 us
    all_to_all x1, waiting for transfers between devices, local(): lax.all_to_all(lax.all_to_all(product, 'pb', split_axis=0, concat_axis=0,...  92.9 us
    all_gather x1, blocking collectives, local(): gathered = lax.all_gather(trial_blocks, 'pb', axis=0, tiled=True)  52.3 us
    unnamed x18, local copies, waits for them, and re-layouts  33.9 us
    all_to_all x3, local copies, waits for them, and re-layouts, local(): lax.all_to_all(lax.all_to_all(product, 'pb', split_axis=0, concat_axis=0,...  32.2 us
    all_to_all x1, other arithmetic, local(): lax.all_to_all(lax.all_to_all(product, 'pb', split_axis=0, concat_axis=0,...  30.1 us
  transfers between devices with their start and end apart: 3, of which 2 were waited for; matrix products, arithmetic and copies ran while one was open for 2% of the time, Pallas kernels for 0%

profile of v1, /device:TPU:8, one launch (start us, length us, event | category | flops | bytes accessed | tf_op | source)
XLA Modules:
  0.0 1028.9 jit_solution(14765611050665016095)
XLA Ops:
  6.5 0.0 copy-start
  6.5 1.0 convert_reduce_fusion
  7.5 0.7 multiply_add_fusion
  8.2 0.1 select_reduce_fusion
  8.3 0.1 reduce_sum.36
  8.4 0.1 fusion.16
  8.6 0.1 broadcast_in_dim.68
  8.7 5.8 gather_fusion
  14.5 4.0 select_select_fusion
  18.4 0.0 copy-start.5
  18.5 198.0 %all_to_all.25 = f32[64,2,16,1024]{3,2,1,0:T(8,128)S(1)} all-to-all(f32[64,2,16,1024]{3,2,1,0:T(8,128)S(1)} %select_select_fusion), channel_id=1, replica_groups=mesh['pb'=64,'ka'=4] {'pb'}, dimensions={0} | all-to-all | bytes 16777216 | tf_op jit(solution)/shard_map/all_to_all | solution.py:28
  216.4 0.0 copy-done.5
  216.4 27.7 %fusion = f32[64,2,16,1024]{3,2,1,0:T(8,128)S(1)} fusion(f32[64,2,16,1024]{3,2,1,0:T(8,128)S(1)} %all_to_all.25, f32[1,1024,1024]{2,1,0:T(8,128)S(1)} %copy-done.5), kind=kOutput, calls=%fused_computation.8 | convolution fusion | flops 25769803776 | bytes 20971520 | tf_op jit(solution)/shard_map/scrg,gh->scrh/dot_general | solution.py:26
  244.1 192.2 %all_to_all.26 = f32[64,2,16,1024]{3,2,1,0:T(8,128)} all-to-all(f32[64,2,16,1024]{3,2,1,0:T(8,128)S(1)} %fusion), channel_id=1, replica_groups=mesh['pb'=64,'ka'=4] {'pb'}, dimensions={0} | all-to-all | bytes 16777216 | tf_op jit(solution)/shard_map/all_to_all | solution.py:34
  436.3 16.3 %copy.59 = f32[64,2,16,1024]{0,2,1,3:T(8,128)} copy(f32[64,2,16,1024]{3,2,1,0:T(8,128)} %all_to_all.26) | data formatting | bytes 16777216 | tf_op jit(solution)/shard_map/all_to_all | solution.py:34
  452.6 14.3 %reshape.143 = f32[4,1,524288]{2,1,0:T(1,128)} reshape(f32[1024,2,16,64]{3,2,1,0:T(8,128)} %bitcast.69) | data formatting | bytes 16777216
  466.9 0.0 copy-start.4
  466.9 6.2 all-to-all-start.2
  473.1 0.0 all-gather.4.cloned.1.call-start
  473.1 0.0 copy-done.4
  473.1 92.9 %all-to-all-done.2 = f32[4,1,524288]{2,1,0:T(1,128)} async-done(((f32[4,1,524288]{2,1,0:T(1,128)}), f32[4,1,524288]{2,1,0:T(1,128)}, u32[]{:S(2)}, u32[]{:S(2)}) %all-to-all-start.2) | async-done | bytes 8388640 | tf_op jit(solution)/shard_map/all_to_all | solution.py:33
  566.0 0.5 broadcast.181
  566.6 30.1 %reduce = f32[4,524288]{1,0:T(4,128)} reduce(f32[4,1,524288]{2,1,0:T(1,128)} %all-to-all-done.2, f32[]{:T(128)} %broadcast.181), dimensions={1}, to_apply=%all_to_all.19.reduce_sub_computation | reduce | bytes 16777220 | tf_op jit(solution)/shard_map/all_to_all | solution.py:33
  596.7 16.8 %reshape.144 = f32[1024,2,16,64]{3,2,1,0:T(8,128)} reshape(f32[4,524288]{1,0:T(4,128)} %reduce) | data formatting | bytes 16777216
  613.5 23.1 %copy.73 = f32[64,2,16,4,256]{4,3,2,1,0:T(4,128)} copy(f32[64,2,16,4,256]{0,2,1,4,3:T(8,128)} %bitcast.70) | data formatting | bytes 16777216 | tf_op jit(solution)/shard_map/all_to_all | solution.py:33
  636.5 8.6 copy.61
  645.1 5.3 gather_fusion.1
  650.4 0.0 copy-done
  650.4 0.0 copy-start.3
  650.4 0.0 copy-start.1
  650.4 0.0 copy-start.2
  650.4 5.4 fusion.2
  655.8 0.0 all-gather.4.cloned.1.call-update
  655.8 0.0 all-reduce.3.cloned.1.call-start
  655.9 0.0 copy-done.3
  655.9 0.0 copy-done.1
  655.9 0.7 gather_fusion.2
  656.6 0.7 gather_fusion.3
  657.3 0.0 copy-done.2
  657.3 52.3 %all-gather.1 = f32[64,1,3584]{2,1,0:T(1,128)} all-gather(f32[1,1,3584]{2,1,0:T(1,128)S(1)} %bitcast.77), channel_id=1, replica_groups=mesh['pb'=64,'ka'=4] {'pb'}, dimensions={0}, use_global_device_ids=true | all-gather | bytes 931840 | tf_op jit(solution)/shard_map/all_gather | solution.py:48
  709.7 3.9 copy.57
  713.6 2.6 reshape.68
  716.2 5.5 copy.58
  721.7 3.8 gather_fusion.4
  725.6 3.8 gather_fusion.5
  729.4 0.0 all-gather.4.cloned.1.call-done
  729.4 5.1 reduce_sum.38
  734.5 5.7 copy.62
  740.2 14.5 %copy.63 = f32[26,8,8,14,14]{3,2,4,1,0:T(8,128)} copy(f32[26,8,8,14,14]{0,2,1,4,3:T(8,128)} %bitcast.71) | data formatting | bytes 2609152 | tf_op jit(solution)/shard_map/reshape | solution.py:56
  754.7 14.6 %copy.66 = f32[26,8,8,14,14]{4,1,3,2,0:T(8,128)} copy(f32[26,8,8,14,14]{0,2,1,4,3:T(8,128)} %bitcast.72) | data formatting | bytes 2609152 | tf_op jit(solution)/shard_map/reshape | solution.py:56
  769.3 23.0 %convolution_bitcast_fusion.1 = f32[26,32,8,14]{1,3,2,0:T(8,128)} fusion(f32[26,8,8,14,14]{3,2,4,1,0:T(8,128)} %copy.63, f32[26,32,8,14]{1,2,3,0:T(8,128)} %gather_fusion.4, pred[26]{0:T(512)(128)(4,1)S(1)} %get-tuple-element.13), kind=kOutput, calls=%fused_computation.13 | convolution fusion | flops 125332480 | bytes 2050074 | tf_op jit(solution)/shard_map/pvwcd,pnwd->pnvc/dot_general | solution.py:57
  792.3 3.7 copy.64
  796.0 4.0 reshape.71
  800.0 1.4 fusion.14
  801.5 23.0 %convolution_bitcast_fusion = f32[26,32,8,14]{1,3,2,0:T(8,128)} fusion(f32[26,8,8,14,14]{4,1,3,2,0:T(8,128)} %copy.66, f32[26,32,8,14]{1,2,3,0:T(8,128)} %gather_fusion.5, pred[26]{0:T(512)(128)(4,1)S(1)} %get-tuple-element.6), kind=kOutput, calls=%fused_computation.12 | convolution fusion | flops 125332480 | bytes 2050074 | tf_op jit(solution)/shard_map/pvwcd,pnvc->pnwd/dot_general | solution.py:58
  824.5 3.7 copy.67
  828.2 0.0 copy-start.6
  828.2 4.0 reshape.72
  832.2 2.6 convolution_add_fusion
  834.8 0.0 all-reduce.3.cloned.1.call-update
  834.8 0.0 copy-done.6
  834.8 0.6 dynamic-slice
  835.5 184.0 %all-reduce.3.cloned.1.call-done = f32[64,3584]{1,0:T(8,128)} async-done(((f32[64,3584]{1,0:T(8,128)}), f32[64,3584]{1,0:T(8,128)}) %all-reduce.3.cloned.1.call-update) | async-done | bytes 917520
  1019.5 2.1 constant_dynamic-slice_fusion
  (12 shorter events, 0.1 us)
Async XLA Ops:
  6.5 643.9 %copy-start = (bf16[26,196,256]{2,1,0:T(8,128)(2,1)S(1)}, bf16[26,196,256]{2,1,0:T(8,128)(2,1)}, u32[]{:S(2)}) copy-start(bf16[26,196,256]{2,1,0:T(8,128)(2,1)} %param.12) | copy-start | bytes 7827460
  18.4 198.0 %copy-start.5 = (f32[1,1024,1024]{2,1,0:T(8,128)S(1)}, f32[1,1024,1024]{2,1,0:T(8,128)}, u32[]{:S(2)}) copy-start(f32[1,1024,1024]{2,1,0:T(8,128)} %param.13) | copy-start | bytes 12582916
  466.9 6.2 copy-start.4
  466.9 99.1 %all-to-all-start.2 = ((f32[4,1,524288]{2,1,0:T(1,128)}), f32[4,1,524288]{2,1,0:T(1,128)}, u32[]{:S(2)}, u32[]{:S(2)}) async-start(f32[4,1,524288]{2,1,0:T(1,128)} %reshape.143), calls=%async_computation.2 | async-start | bytes 16777216 | tf_op jit(solution)/shard_map/all_to_all | solution.py:33
  473.1 256.3 %all-gather.4.cloned.1.call-start = ((), (), s32[]{:S(2)}) async-start(), calls=%async_computation.3 | async-start | bytes 8519680 | tf_op jit(solution)/shard_map/all_gather | solution.py:46
  650.4 5.5 copy-start.3
  650.4 5.5 copy-start.1
  650.4 6.9 copy-start.2
  655.8 363.7 %all-reduce.3.cloned.1.call-start = ((), (), s32[]{:S(2)}) async-start(), calls=%async_computation.4 | async-start | bytes 1835008
  828.2 6.6 copy-start.6
Sparse Core Ops, SparseCore 0:
  655.9 67.7 all-gather.3
  834.9 184.5 all-reduce.2
